TPU v7x, 256 devices: a whole 4x4x8 slice. The times are simulated.
256 devices in a mesh: hyp: 4 (over z_lo), row: 16 (over x, z_hi, core), col: 4 (over y).
Axes of the slice: x: 4, y: 4, z: 8 (z_hi: 2, z_lo: 4; z = z_hi * 4 + z_lo), core: 2. Of those that a mesh axis runs over, the one named last changes fastest.
Arguments:
- front_orig: bfloat16 [40960, 10240], P(('hyp', 'row'), 'col'), parts along dimension 0, as said below
- child_updates: bfloat16 [65536, 8192], P(('hyp', 'row'), 'col'), parts along dimension 0, as said below
- child_map: int32 [8, 64], P('hyp'), parts along dimension 0, may hold values from 0 to 79, as said below
- panel_inverse: bfloat16 [1024, 256], P('hyp'), parts along dimension 0, as said below
Outputs:
- schur: bfloat16 [40960, 10240], P(('hyp', 'row'), 'col'), parts along dimension 0
- panel: bfloat16 [40960, 256], P(('hyp', 'row')), parts along dimension 0
There are 4 independent parts, one for each index of `hyp`. A program takes and returns all parts, laid end to end along the dimension named above; each array names one. Nothing has to cross between parts.
Inputs may be any that keep to these rules, and one draw needn't show every extreme that they name: `child_map`: each child's entries are distinct. Parent block p lies on row index p // 5 and column index p // 20. Of the 8 blocks of a child on one row index (child c on row indices c * 8 to (c + 1) * 8 - 1, in order), at most 1 lie on one parent row index; of the 16 blocks on one column index, at most 4 lie on one parent column index. Every parent row index receives the same number of blocks of each child. `child_updates`: each child's update block is symmetric. `front_orig`: Symmetric. `panel_inverse`: upper triangular with a positive diagonal.
All inputs are finite; a program needn't handle non-finite values.
Results may differ from a plain program's by a relative error of at most 0.0052.
Values may be sent and summed in bfloat16 or wider, within the bound.
No kernel may reach another device: no remote copies, remote signals or barrier semaphores. Data moves between devices by JAX's collectives and lax.ppermute only.
A program may use at most 128 MiB of HBM per device.

v0:
```python
import jax
import jax.numpy as jnp
from jax import lax
from jax.sharding import PartitionSpec as P

B = 128
PANEL = 256


def picked(shard, axis, root):
    return lax.dynamic_index_in_dim(lax.all_gather(shard, axis), root, 0, keepdims=False)


def one_hot(indices, columns):
    return (indices[..., None] == jnp.arange(columns, dtype=jnp.int32)).astype(jnp.bfloat16)


def earlier_same(labels):
    length = labels.shape[-1]
    matches = labels[..., :, None] == labels[..., None, :]
    before = jnp.arange(length)[None, :] < jnp.arange(length)[:, None]
    return jnp.sum(matches & before, axis=-1)


def send_table(block_ids, owner_width, capacity, owners_count):
    owners = block_ids // owner_width
    slots = owners * capacity + earlier_same(owners)
    return one_hot(slots, owners_count * capacity)


def receive_table(all_ids, owner_width, my_index, capacity):
    owners = all_ids // owner_width
    rank_in = earlier_same(owners)
    local_block = all_ids - my_index * owner_width
    arrives = (owners == my_index)[:, :, None, None]
    slot_match = rank_in[:, :, None, None] == jnp.arange(capacity)[None, None, :, None]
    block_match = local_block[:, :, None, None] == jnp.arange(owner_width)[None, None, None, :]
    table = jnp.sum(arrives & slot_match & block_match, axis=1)
    return table.reshape(-1, owner_width).astype(jnp.bfloat16)


def local(front_orig, child_updates, child_map, panel_inverse):
    n_row = lax.axis_size("row")
    n_col = lax.axis_size("col")
    me_row = lax.axis_index("row")
    me_col = lax.axis_index("col")
    rows_local, cols_local = child_updates.shape
    part_rows, part_cols = front_orig.shape
    senders = n_row // 2
    child_index = me_row // senders
    blocks_row = rows_local // B
    blocks_col = cols_local // B
    fine_count = max(n_row, n_col)
    parent_row_blocks = part_rows // B
    parent_col_blocks = part_cols // B
    row_cap = max(1, blocks_row // fine_count) * (fine_count // n_row)
    col_cap = max(1, blocks_col // fine_count) * (fine_count // n_col)
    my_map = lax.dynamic_index_in_dim(child_map, child_index, 0, keepdims=False)
    flat_map = child_map.reshape(-1)
    row_ids = lax.dynamic_slice_in_dim(flat_map, me_row * blocks_row, blocks_row)
    row_send = send_table(row_ids, parent_row_blocks, row_cap, n_row)
    row_receive = receive_table(
        child_map.reshape(n_row, blocks_row), parent_row_blocks, me_row, row_cap
    )
    col_ids = lax.dynamic_slice_in_dim(my_map, me_col * blocks_col, blocks_col)
    col_send = send_table(col_ids, parent_col_blocks, col_cap, n_col).reshape(
        blocks_col, n_col, col_cap
    )
    row_pick = row_send.reshape(blocks_row, n_row, row_cap)
    tiles_four = child_updates.reshape(blocks_row, B, blocks_col, B)
    outgoing = jnp.einsum(
        "ibjc,ipa,jqe->pqabec", tiles_four, row_pick, col_send, preferred_element_type=jnp.float32
    ).astype(jnp.bfloat16)
    outgoing = outgoing.reshape(n_row * n_col, row_cap * B, col_cap * B)
    incoming = lax.all_to_all(outgoing, ("row", "col"), split_axis=0, concat_axis=0, tiled=True)
    tiles = incoming.reshape(n_row, n_col, row_cap, B, col_cap, B)
    col_tables = jnp.stack(
        [
            receive_table(
                child_map[k].reshape(n_col, blocks_col), parent_col_blocks, me_col, col_cap
            ).reshape(n_col, col_cap, parent_col_blocks)
            for k in range(2)
        ]
    )
    per_source = jnp.repeat(col_tables, senders, axis=0)
    placed_cols = jnp.einsum(
        "rsabec,rseq->rabqc", tiles, per_source, preferred_element_type=jnp.float32
    ).astype(jnp.bfloat16)
    row_table = row_receive.reshape(n_row, row_cap, parent_row_blocks)
    assembled = jnp.einsum(
        "rabqc,rap->pbqc", placed_cols, row_table, preferred_element_type=jnp.float32
    )
    front32 = assembled.reshape(part_rows, part_cols) + front_orig.astype(jnp.float32)
    front = front32.astype(jnp.bfloat16)
    local_panel = jnp.dot(
        front[:, :PANEL], panel_inverse, preferred_element_type=jnp.float32
    ).astype(jnp.bfloat16)
    row_panel = picked(local_panel, "col", 0)
    all_panel = lax.all_gather(row_panel, "row", axis=0, tiled=True)
    col_panel = lax.dynamic_slice_in_dim(all_panel, me_col * part_cols, part_cols, 0)
    update = lax.dot_general(
        row_panel, col_panel, (((1,), (1,)), ((), ())), preferred_element_type=jnp.float32
    )
    schur = (front.astype(jnp.float32) - update).astype(jnp.bfloat16)
    return (schur, row_panel)


def solution(mesh):
    in_specs = (P(("hyp", "row"), "col"), P(("hyp", "row"), "col"), P("hyp", None), P("hyp", None))
    out_specs = (P(("hyp", "row"), "col"), P(("hyp", "row"), None))
    return jax.shard_map(local, mesh=mesh, in_specs=in_specs, out_specs=out_specs, check_vma=False)
```

profile of v0, /device:TPU:1, one launch (start us, length us, event | category | flops | bytes accessed | tf_op | source)
XLA Modules:
  0.0 411.4 jit_solution(8262552116973549749)
XLA Ops:
  7.2 0.0 copy-start
  7.2 0.8 reshape.440
  8.0 0.1 and_select_fusion
  8.1 0.2 convert_reduce_fusion.7
  8.3 0.1 fusion.30
  8.4 0.8 bitcast_select_fusion
  9.2 0.2 convert_reduce_fusion.6
  9.3 3.6 copy.26
  12.9 1.3 fusion.13
  14.3 8.8 %convert_bitcast_fusion = bf16[16,4,1,128,4,128]{5,0,3,4,1,2:T(8,128)(2,1)} fusion(bf16[4,4,8,128,128]{4,1,3,2,0:T(4,128)(2,1)S(1)} %fusion.13, s32[8]{0:T(128)S(1)} %fusion.30), kind=kOutput, calls=%fused_computation.6 | convolution fusion | flops 67108992 | bytes 12582944 | tf_op jit(solution)/shard_map/ibjc,ipa,jqe->pqabec/dot_general | solution.py:71
  23.1 13.7 %copy.17 = bf16[16,4,1,128,4,128]{3,5,4,1,0,2:T(8,128)(2,1)} copy(bf16[16,4,1,128,4,128]{5,0,3,4,1,2:T(8,128)(2,1)} %convert_bitcast_fusion) | data formatting | bytes 16777216 | tf_op jit(solution)/shard_map/convert_element_type | solution.py:73
  36.8 0.0 copy-start.1
  36.8 15.9 %all-to-all-start = ((bf16[64,128,512]{1,2,0:T(8,128)(2,1)}), bf16[64,128,512]{1,2,0:T(8,128)(2,1)}, u32[]{:S(2)}, u32[]{:S(2)}) async-start(bf16[64,128,512]{1,2,0:T(8,128)(2,1)} %bitcast.62), calls=%async_computation | async-start | bytes 16777216 | tf_op jit(solution)/shard_map/all_to_all | solution.py:75
  52.7 0.2 all-gather.6.cloned.1.call-start
  53.0 0.0 copy-done.1
  53.0 0.1 and.196
  53.1 0.1 and.205
  53.2 0.1 and.189
  53.3 0.1 copy.12
  53.4 0.1 div.95
  53.5 0.1 div.97
  53.6 0.1 sub.77
  53.7 0.1 sub.80
  53.8 0.3 convert_reduce_fusion.3
  54.1 0.1 iota_compare_fusion
  54.2 0.1 convert_reduce_fusion
  54.3 0.1 iota_compare_fusion.1
  54.4 0.1 convert_reduce_fusion.1
  54.6 0.1 div.93
  54.7 0.1 copy.11
  54.7 0.1 sub.73
  54.8 0.1 copy.14
  54.9 0.1 convert_reduce_fusion.4
  55.0 183.0 %all-to-all-done = bf16[64,128,512]{1,2,0:T(8,128)(2,1)} async-done(((bf16[64,128,512]{1,2,0:T(8,128)(2,1)}), bf16[64,128,512]{1,2,0:T(8,128)(2,1)}, u32[]{:S(2)}, u32[]{:S(2)}) %all-to-all-start) | async-done | bytes 8388640 | tf_op jit(solution)/shard_map/all_to_all | solution.py:75
  238.0 14.6 %copy.18 = bf16[16,4,128,4,128]{4,1,3,2,0:T(4,128)(2,1)} copy(bf16[16,4,128,4,128]{2,4,3,1,0:T(8,128)(2,1)} %bitcast.17) | data formatting | bytes 16777216 | tf_op jit(solution)/shard_map/reshape.31
  252.6 12.2 %fusion = bf16[16,128,20,128]{3,2,1,0:T(8,128)(2,1)} fusion(bf16[16,4,4,20,1]{3,1,2,4,0:T(4,128)(2,1)S(1)} %bitcast.66, bf16[16,4,128,4,128]{4,1,3,2,0:T(4,128)(2,1)} %copy.18), kind=kOutput, calls=%fused_computation.1 | convolution fusion | flops 173015040 | bytes 18884608 | tf_op jit(solution)/shard_map/rsabec,rseq->rabqc/dot_general | solution.py:86
  264.8 11.1 %fusion.1 = f32[5,128,20,128]{3,0,2,1:T(8,128)S(1)} fusion(bf16[16,128,20,128]{3,2,1,0:T(8,128)(2,1)} %fusion, s32[16,5]{0,1:T(8,128)S(1)} %convert_reduce_fusion.5), kind=kOutput, calls=%fused_computation.2 | convolution fusion | flops 52428880 | bytes 17039680 | tf_op jit(solution)/shard_map/rabqc,rap->pbqc/dot_general | solution.py:90
  275.9 1.3 copy.20
  277.3 3.5 fusion.7
  280.8 0.0 copy-done
  280.8 1.0 convolution_convert_fusion
  281.8 0.0 all-gather.6.cloned.1.call-update
  281.8 0.0 all-gather.8.cloned.1.call-start
  281.8 28.4 %all-gather.6.cloned.1.call-done = bf16[2560,256]{1,0:T(8,128)(2,1)} async-done(((bf16[640,256]{1,0:T(8,128)(2,1)}), bf16[2560,256]{1,0:T(8,128)(2,1)}) %all-gather.6.cloned.1.call-update) | async-done | bytes 1310736 | tf_op jit(solution)/shard_map/all_gather | solution.py:11
  310.2 1.7 slice.15
  311.9 0.0 all-gather.8.cloned.1.call-update
  312.0 88.4 %all-gather.8.cloned.1.call-done = bf16[10240,256]{1,0:T(8,128)(2,1)} async-done(((bf16[640,256]{1,0:T(8,128)(2,1)}), bf16[10240,256]{1,0:T(8,128)(2,1)}) %all-gather.8.cloned.1.call-update) | async-done | bytes 5242896 | tf_op jit(solution)/shard_map/all_gather | solution.py:99
  400.3 4.2 %subtract_convert_fusion = bf16[640,2560]{1,0:T(8,128)(2,1)} fusion(bf16[640,2560]{1,0:T(8,128)(2,1)S(1)} %fusion.7, bf16[640,256]{1,0:T(8,128)(2,1)} %slice.15, bf16[10240,256]{1,0:T(8,128)(2,1)} %all-gather.8.cloned.1.call-done, s32[]{:T(128)S(6)} %select_n.105), kind=kOutput, calls=%fused_computation.9 | convolution fusion | flops 843776000 | bytes 8192004 | tf_op jit(solution)/shard_map/dot_general | solution.py:101
  (20 shorter events, 0.2 us)
Async XLA Ops:
  7.2 273.6 %copy-start = (bf16[256,256]{1,0:T(8,128)(2,1)S(1)}, bf16[256,256]{1,0:T(8,128)(2,1)}, u32[]{:S(2)}) copy-start(bf16[256,256]{1,0:T(8,128)(2,1)} %param.7) | copy-start | bytes 393220
  36.8 16.2 %copy-start.1 = (s32[2,64]{1,0:T(2,128)S(1)}, s32[2,64]{1,0:T(2,128)}, u32[]{:S(2)}) copy-start(s32[2,64]{1,0:T(2,128)} %param.6) | copy-start | bytes 1540
  36.8 201.2 %all-to-all-start = ((bf16[64,128,512]{1,2,0:T(8,128)(2,1)}), bf16[64,128,512]{1,2,0:T(8,128)(2,1)}, u32[]{:S(2)}, u32[]{:S(2)}) async-start(bf16[64,128,512]{1,2,0:T(8,128)(2,1)} %bitcast.62), calls=%async_computation | async-start | bytes 16777216 | tf_op jit(solution)/shard_map/all_to_all | solution.py:75
  52.7 257.5 %all-gather.6.cloned.1.call-start = ((), (), s32[]{:S(2)}) async-start(), calls=%async_computation.1 | async-start | bytes 1638400 | tf_op jit(solution)/shard_map/all_gather | solution.py:11
  281.8 118.6 %all-gather.8.cloned.1.call-start = ((), (), s32[]{:S(2)}) async-start(), calls=%async_computation.2 | async-start | bytes 5570560 | tf_op jit(solution)/shard_map/all_gather | solution.py:99
Sparse Core Ops, SparseCore 0:
  281.9 28.2 all-gather.5
  313.5 86.8 all-gather.7
where the time goes:
time: 412 us; the launch traced here: 411 us
  waiting for transfers between devices  300 us (73%)
  matrix products  38.6 us (9%)
  local copies, waits for them, and re-layouts  36.8 us (9%)
  starting transfers between devices  16.2 us (4%)
  between operations  14.3 us (3%)
  other arithmetic  5.78 us (1%)
    all_to_all x1, waiting for transfers between devices, local(): lax.all_to_all(outgoing, ('row', 'col'), split_axis=0, concat_axis=0, til...  183 us
    all_gather x1, waiting for transfers between devices, local(): all_panel = lax.all_gather(row_panel, 'row', axis=0, tiled=True)  88.4 us
    all_gather x1, waiting for transfers between devices, picked(): lax.all_gather(shard, axis)  28.4 us
    all_to_all x1, starting transfers between devices, local(): lax.all_to_all(outgoing, ('row', 'col'), split_axis=0, concat_axis=0, til...  15.9 us
    another operation x1, local copies, waits for them, and re-layouts  14.6 us
    convert_element_type x1, local copies, waits for them, and re-layouts, local(): outgoing = jnp.einsum('ibjc,ipa,jqe->pqabec', tiles_four, row_pick, col_s...  13.7 us
    dot_general x1, matrix products, local(): jnp.einsum('rsabec,rseq->rabqc', tiles, per_source, preferred_element_typ...  12.2 us
    dot_general x1, matrix products, local(): jnp.einsum('rabqc,rap->pbqc', placed_cols, row_table, preferred_element_t...  11.1 us
  transfers between devices with their start and end apart: 3, of which 3 were waited for; matrix products, arithmetic and copies ran while one was open for 0% of the time, Pallas kernels for 0%

commit v1 on v0

--- a/solution.py
+++ b/solution.py
@@ -96,7 +96,9 @@
         front[:, :PANEL], panel_inverse, preferred_element_type=jnp.float32
     ).astype(jnp.bfloat16)
     row_panel = picked(local_panel, "col", 0)
-    all_panel = lax.all_gather(row_panel, "row", axis=0, tiled=True)
+    all_panel = jnp.concatenate(
+        lax.all_to_all(jnp.stack([row_panel] * lax.axis_size("row")), "row", 0, 0), axis=0
+    )
     col_panel = lax.dynamic_slice_in_dim(all_panel, me_col * part_cols, part_cols, 0)
     update = lax.dot_general(
         row_panel, col_panel, (((1,), (1,)), ((), ())), preferred_element_type=jnp.float32

time: 412 us -> 461 us (1.12)
  waiting for transfers between devices: 300 us -> 332 us
  starting transfers between devices: 16.2 us -> 27.4 us
    all_to_all x0 -> x1, waiting for transfers between devices: none -> 121 us  [local(): lax.all_to_all(jnp.stack([row_panel] * lax.axis_size('row')), 'row', 0, 0)]
    all_gather x1 -> x0, waiting for transfers between devices: 88.4 us -> none  [local(): all_panel = lax.all_gather(row_panel, 'row', axis=0, tiled=True)]
    all_to_all x0 -> x1, starting transfers between devices: none -> 11.5 us  [local(): lax.all_to_all(jnp.stack([row_panel] * lax.axis_size('row')), 'row', 0, 0)]
    another operation x1 -> x2, local copies, waits for them, and re-layouts: 14.6 us -> 17.4 us
where the time goes in v1:
time: 461 us; the launch traced here: 460 us
  waiting for transfers between devices  332 us (72%)
  local copies, waits for them, and re-layouts  41.3 us (9%)
  matrix products  38.6 us (8%)
  starting transfers between devices  27.4 us (6%)
  between operations  14.3 us (3%)
  other arithmetic  5.78 us (1%)
    all_to_all x1, waiting for transfers between devices, local(): lax.all_to_all(outgoing, ('row', 'col'), split_axis=0, concat_axis=0, til...  183 us
    all_to_all x1, waiting for transfers between devices, local(): lax.all_to_all(jnp.stack([row_panel] * lax.axis_size('row')), 'row', 0, 0)  121 us
    all_gather x1, waiting for transfers between devices, picked(): lax.all_gather(shard, axis)  28.4 us
    all_to_all x1, starting transfers between devices, local(): lax.all_to_all(outgoing, ('row', 'col'), split_axis=0, concat_axis=0, til...  15.9 us
    another operation x1, local copies, waits for them, and re-layouts  14.6 us
    convert_element_type x1, local copies, waits for them, and re-layouts, local(): outgoing = jnp.einsum('ibjc,ipa,jqe->pqabec', tiles_four, row_pick, col_s...  13.7 us
    dot_general x1, matrix products, local(): jnp.einsum('rsabec,rseq->rabqc', tiles, per_source, preferred_element_typ...  12.2 us
    all_to_all x1, starting transfers between devices, local(): lax.all_to_all(jnp.stack([row_panel] * lax.axis_size('row')), 'row', 0, 0)  11.5 us
  transfers between devices with their start and end apart: 3, of which 3 were waited for; matrix products, arithmetic and copies ran while one was open for 0% of the time, Pallas kernels for 0%

profile of v1, /device:TPU:1, one launch (start us, length us, event | category | flops | bytes accessed | tf_op | source)
XLA Modules:
  0.0 459.8 jit_solution(9858955027390113560)
XLA Ops:
  7.2 0.0 copy-start
  7.2 0.8 reshape.444
  8.0 0.1 and_select_fusion
  8.1 0.2 convert_reduce_fusion.7
  8.3 0.1 fusion.30
  8.4 0.8 bitcast_select_fusion
  9.2 0.2 convert_reduce_fusion.6
  9.3 3.6 copy.26
  12.9 1.3 fusion.13
  14.3 8.8 %convert_bitcast_fusion = bf16[16,4,1,128,4,128]{5,0,3,4,1,2:T(8,128)(2,1)} fusion(bf16[4,4,8,128,128]{4,1,3,2,0:T(4,128)(2,1)S(1)} %fusion.13, s32[8]{0:T(128)S(1)} %fusion.30), kind=kOutput, calls=%fused_computation.6 | convolution fusion | flops 67108992 | bytes 12582944 | tf_op jit(solution)/shard_map/ibjc,ipa,jqe->pqabec/dot_general | solution.py:71
  23.1 13.7 %copy.17 = bf16[16,4,1,128,4,128]{3,5,4,1,0,2:T(8,128)(2,1)} copy(bf16[16,4,1,128,4,128]{5,0,3,4,1,2:T(8,128)(2,1)} %convert_bitcast_fusion) | data formatting | bytes 16777216 | tf_op jit(solution)/shard_map/convert_element_type | solution.py:73
  36.8 15.9 %all-to-all-start = ((bf16[64,128,512]{1,2,0:T(8,128)(2,1)}), bf16[64,128,512]{1,2,0:T(8,128)(2,1)}, u32[]{:S(2)}, u32[]{:S(2)}) async-start(bf16[64,128,512]{1,2,0:T(8,128)(2,1)} %bitcast.63), calls=%async_computation | async-start | bytes 16777216 | tf_op jit(solution)/shard_map/all_to_all | solution.py:75
  52.7 0.0 all-gather.3.cloned.1.call-start
  52.8 0.1 and.196
  52.9 0.1 and.205
  53.0 0.1 and.189
  53.1 0.1 copy.12
  53.2 0.1 div.95
  53.3 0.1 div.97
  53.4 0.1 sub.77
  53.5 0.1 sub.80
  53.6 0.3 convert_reduce_fusion.3
  53.9 0.1 iota_compare_fusion
  54.0 0.1 convert_reduce_fusion
  54.1 0.1 iota_compare_fusion.1
  54.2 0.1 convert_reduce_fusion.1
  54.4 0.1 div.93
  54.5 0.1 copy.11
  54.6 0.1 sub.73
  54.6 0.1 copy.14
  54.7 0.1 convert_reduce_fusion.4
  54.9 183.1 %all-to-all-done = bf16[64,128,512]{1,2,0:T(8,128)(2,1)} async-done(((bf16[64,128,512]{1,2,0:T(8,128)(2,1)}), bf16[64,128,512]{1,2,0:T(8,128)(2,1)}, u32[]{:S(2)}, u32[]{:S(2)}) %all-to-all-start) | async-done | bytes 8388640 | tf_op jit(solution)/shard_map/all_to_all | solution.py:75
  238.0 14.6 %copy.18 = bf16[16,4,128,4,128]{4,1,3,2,0:T(4,128)(2,1)} copy(bf16[16,4,128,4,128]{2,4,3,1,0:T(8,128)(2,1)} %bitcast.17) | data formatting | bytes 16777216 | tf_op jit(solution)/shard_map/reshape.32
  252.6 12.2 %fusion = bf16[16,128,20,128]{3,2,1,0:T(8,128)(2,1)} fusion(bf16[16,4,4,20,1]{3,1,2,4,0:T(4,128)(2,1)S(1)} %bitcast.67, bf16[16,4,128,4,128]{4,1,3,2,0:T(4,128)(2,1)} %copy.18), kind=kOutput, calls=%fused_computation.1 | convolution fusion | flops 173015040 | bytes 18884608 | tf_op jit(solution)/shard_map/rsabec,rseq->rabqc/dot_general | solution.py:86
  264.8 11.1 %fusion.1 = f32[5,128,20,128]{3,0,2,1:T(8,128)S(1)} fusion(bf16[16,128,20,128]{3,2,1,0:T(8,128)(2,1)} %fusion, s32[16,5]{0,1:T(8,128)S(1)} %convert_reduce_fusion.5), kind=kOutput, calls=%fused_computation.2 | convolution fusion | flops 52428880 | bytes 17039680 | tf_op jit(solution)/shard_map/rabqc,rap->pbqc/dot_general | solution.py:90
  275.9 1.3 copy.20
  277.3 3.5 fusion.7
  280.8 0.0 copy-start.1
  280.8 1.7 copy-done.1
  282.5 1.0 convolution_convert_fusion
  283.5 0.0 all-gather.3.cloned.1.call-update
  283.5 28.4 %all-gather.3.cloned.1.call-done = bf16[2560,256]{1,0:T(8,128)(2,1)} async-done(((bf16[640,256]{1,0:T(8,128)(2,1)}), bf16[2560,256]{1,0:T(8,128)(2,1)}) %all-gather.3.cloned.1.call-update) | async-done | bytes 1310736 | tf_op jit(solution)/shard_map/all_gather | solution.py:11
  311.9 1.0 slice.15
  312.9 0.7 copy-done.3
  313.6 2.9 stack.5
  316.5 11.5 %all-to-all-start.1 = ((bf16[16,640,256]{2,1,0:T(8,128)(2,1)}), bf16[16,640,256]{2,1,0:T(8,128)(2,1)}, u32[]{:S(2)}, u32[]{:S(2)}) async-start(bf16[16,640,256]{2,1,0:T(8,128)(2,1)} %stack.5), calls=%async_computation.1 | async-start | bytes 10485760 | tf_op jit(solution)/shard_map/all_to_all | solution.py:100
  328.0 120.8 %all-to-all-done.1 = bf16[16,640,256]{2,1,0:T(8,128)(2,1)} async-done(((bf16[16,640,256]{2,1,0:T(8,128)(2,1)}), bf16[16,640,256]{2,1,0:T(8,128)(2,1)}, u32[]{:S(2)}, u32[]{:S(2)}) %all-to-all-start.1) | async-done | bytes 5242912 | tf_op jit(solution)/shard_map/all_to_all | solution.py:100
  448.8 4.2 subtract_convert_fusion
  (26 shorter events, 0.3 us)
Async XLA Ops:
  7.2 275.3 %copy-start = (bf16[256,256]{1,0:T(8,128)(2,1)S(1)}, bf16[256,256]{1,0:T(8,128)(2,1)}, u32[]{:S(2)}) copy-start(bf16[256,256]{1,0:T(8,128)(2,1)} %param.7) | copy-start | bytes 393220
  36.8 16.0 %copy-start.4 = (s32[2,64]{1,0:T(2,128)S(1)}, s32[2,64]{1,0:T(2,128)}, u32[]{:S(2)}) copy-start(s32[2,64]{1,0:T(2,128)} %param.6) | copy-start | bytes 1540
  36.8 201.2 %all-to-all-start = ((bf16[64,128,512]{1,2,0:T(8,128)(2,1)}), bf16[64,128,512]{1,2,0:T(8,128)(2,1)}, u32[]{:S(2)}, u32[]{:S(2)}) async-start(bf16[64,128,512]{1,2,0:T(8,128)(2,1)} %bitcast.63), calls=%async_computation | async-start | bytes 16777216 | tf_op jit(solution)/shard_map/all_to_all | solution.py:75
  52.7 259.2 %all-gather.3.cloned.1.call-start = ((), (), s32[]{:S(2)}) async-start(), calls=%async_computation.2 | async-start | bytes 1638400 | tf_op jit(solution)/shard_map/all_gather | solution.py:11
  280.8 1.7 copy-start.1
  312.9 0.7 copy-start.3
  316.5 132.3 %copy-start.2 = (bf16[640,2560]{1,0:T(8,128)(2,1)S(1)}, bf16[640,2560]{1,0:T(8,128)(2,1)}, u32[]{:S(2)}) copy-start(bf16[640,2560]{1,0:T(8,128)(2,1)} %copy-done.1) | copy-start | bytes 9830404
  316.5 132.3 %all-to-all-start.1 = ((bf16[16,640,256]{2,1,0:T(8,128)(2,1)}), bf16[16,640,256]{2,1,0:T(8,128)(2,1)}, u32[]{:S(2)}, u32[]{:S(2)}) async-start(bf16[16,640,256]{2,1,0:T(8,128)(2,1)} %stack.5), calls=%async_computation.1 | async-start | bytes 10485760 | tf_op jit(solution)/shard_map/all_to_all | solution.py:100
Sparse Core Ops, SparseCore 0:
  283.6 28.2 all-gather.2
